TPU v7x, 512 devices: a whole 4x8x8 slice. The times are simulated.
512 devices in a mesh: band: 8 (over x, z_lo), tm: 64 (over y, z_hi, core).
Axes of the slice: x: 4, y: 8, z: 8 (z_hi: 4, z_lo: 2; z = z_hi * 2 + z_lo), core: 2. Of those that a mesh axis runs over, the one named last changes fastest.
Arguments:
- driven_wave: bfloat16 [2048, 2048], P('tm', 'band'), may hold values from -6 to 6
- responses: bfloat16 [1024, 512, 2048], P('tm', None, 'band'), may hold values from -0.01171875 to 0.01171875
- tap_counts: int32 [2048], P('band'), may hold values from 256 to 1024
- panel_links: int32 [2048, 2], P('band'), may hold values 0 or 1
Outputs:
- far_end: bfloat16 [1024, 2048], P('tm', 'band')
All inputs are finite; a program needn't handle non-finite values. No bound on the sum of `panel_links` on one device may be relied on, other than what follows from the above.
Results may differ from a plain program's by a relative error of at most 0.00155.
Values may be sent and summed in bfloat16 or wider, within the bound.
No kernel may reach another device: no remote copies, remote signals or barrier semaphores. Data moves between devices by JAX's collectives and lax.ppermute only.
A program may use at most 64 MiB of HBM per device.

v0:
```python
import jax
import jax.numpy as jnp
from jax import lax
from jax.sharding import PartitionSpec as P

SAMP_DEV = 16


def extended(cells, sides, width):
    for axis, dim in sides:
        count = lax.axis_size(axis)
        ends = count - 1
        head = lax.slice_in_dim(cells, 0, width, axis=dim)
        tail = lax.slice_in_dim(cells, cells.shape[dim] - width, cells.shape[dim], axis=dim)
        cells = jnp.concatenate(
            [
                lax.ppermute(tail, axis, [(i, (i + 1) % count) for i in range(ends)]),
                cells,
                lax.ppermute(head, axis, [((i + 1) % count, i) for i in range(ends)]),
            ],
            axis=dim,
        )
    return cells


def masked_weights(responses, tap_counts, panel_links, first_tap):
    tap_dev, coupled_ports, group_ports = responses.shape
    half_width = (coupled_ports - group_ports) // 2
    tap_index = first_tap + jnp.arange(tap_dev, dtype=jnp.int32)
    tap_alive = tap_index[:, None] < tap_counts[None, :]
    port_index = jnp.arange(coupled_ports, dtype=jnp.int32)[:, None]
    lower_open = panel_links[None, :, 0] == 1
    upper_open = panel_links[None, :, 1] == 1
    couple_open = jnp.where(
        port_index < half_width,
        lower_open,
        jnp.where(port_index >= half_width + group_ports, upper_open, True),
    )
    keep_mask = tap_alive[:, None, :] & couple_open[None, :, :]
    return jnp.where(keep_mask, responses, jnp.zeros_like(responses))


def per_device(driven_wave, responses, tap_counts, panel_links):
    tap_dev = responses.shape[0]
    group_ports = driven_wave.shape[1]
    coupled_ports = 2 * group_ports
    half_width = group_ports // 2
    total_taps = tap_dev * lax.axis_size("tm")
    first_tap = lax.axis_index("tm") * tap_dev
    weights = masked_weights(responses, tap_counts, panel_links, first_tap)
    widened = extended(driven_wave, (("band", 1),), half_width)
    history = lax.all_gather(widened, "tm", axis=0, tiled=True)
    block_count = tap_dev // 8
    first_row = jnp.int32(0)

    def add_block(block_index, running):
        lead_tap = (8 * block_index).astype(jnp.int32)
        offset = first_row + total_taps - first_tap - lead_tap - 7
        window = lax.dynamic_slice_in_dim(history, offset, lax.axis_size("tm") * SAMP_DEV + 7, 0)
        stacked = jnp.concatenate(
            [
                window[7 - shift_index : 7 - shift_index + lax.axis_size("tm") * SAMP_DEV]
                for shift_index in range(8)
            ],
            axis=1,
        )
        tap_panel = lax.dynamic_slice_in_dim(weights, lead_tap, 8, 0).reshape(
            8 * coupled_ports, group_ports
        )
        return running + jnp.dot(stacked, tap_panel, preferred_element_type=jnp.float32)

    summed = lax.psum_scatter(
        lax.fori_loop(
            0,
            block_count,
            add_block,
            jnp.zeros((lax.axis_size("tm") * SAMP_DEV, group_ports), jnp.float32),
        ),
        "tm",
        scatter_dimension=0,
        tiled=True,
    )
    return summed.astype(jnp.bfloat16)


def solution(mesh):
    return jax.shard_map(
        per_device,
        mesh=mesh,
        in_specs=(P("tm", "band"), P("tm", None, "band"), P("band"), P("band", None)),
        out_specs=P("tm", "band"),
        check_vma=False,
    )
```

profile of v0, /device:TPU:2, one launch (start us, length us, event | category | flops | bytes accessed | tf_op | source)
XLA Modules:
  0.0 309.9 jit_solution(17289685736764098820)
XLA Ops:
  7.3 4.3 %collective-permute-start = (bf16[32,128]{1,0:T(8,128)(2,1)S(1)}, bf16[32,128]{1,0:T(8,128)(2,1)S(1)}, u32[]{:S(2)}, u32[]{:S(2)}) collective-permute-start(bf16[32,128]{1,0:T(8,128)(2,1)S(1)} %get-tuple-element.208), channel_id=1, source_target_pairs={{0,64},{64,128},{128,192},{192,256},{256,320},{320,384},{384,448},... | collective-permute-start | bytes 24584 | tf_op jit(solution)/shard_map/ppermute | solution.py:17
  11.5 2.5 collective-permute-start.1
  14.0 3.1 collective-permute-done.1
  17.1 1.3 pad_maximum_fusion
  18.5 0.8 compare_reduce_fusion.1
  19.3 0.8 broadcast_compare_fusion
  20.3 5.4 %and_select_fusion = bf16[16,512,256]{2,1,0:T(8,128)(2,1)} fusion(bf16[16,512,256]{2,1,0:T(8,128)(2,1)} %param.7, pred[512,256]{1,0:T(8,128)(4,1)S(1)} %select_select_fusion, pred[16,256]{1,0:T(8,128)(4,1)S(1)} %broadcast_compare_fusion), kind=kLoop, calls=%fused_computation.10 | loop fusion | flops 4194304 | bytes 8523776 | tf_op jit(solution)/shard_map/jit(_where)/select_n | solution.py:40
  25.7 82.2 %all-gather.2.cloned.1.call-done = bf16[2048,512]{1,0:T(8,128)(2,1)} async-done(((bf16[32,512]{1,0:T(8,128)(2,1)}), bf16[2048,512]{1,0:T(8,128)(2,1)}) %all-gather.2.cloned.1.call-update) | async-done | bytes 2097168 | tf_op jit(solution)/shard_map/all_gather | solution.py:52
  107.8 46.4 %while.18 = (s32[]{:T(128)}, f32[1024,256]{1,0:T(8,128)S(1)}, s32[]{:T(128)}, bf16[2048,512]{1,0:T(8,128)(2,1)}, bf16[16,512,256]{2,1,0:T(8,128)(2,1)}, /*index=...) while((s32[]{:T(128)}, f32[1024,256]{1,0:T(8,128)S(1)}, ...), condition=%wide.region_1.2_spmd.clone, body=%wide.region_0.1_spmd.clone.sunk | while | flops 2148007936 | bytes 41943464 | solution.py:73
  107.8 2.5 dynamic-slice_dynamic-update-slice_fusion.16
  110.3 2.5 dynamic-slice_dynamic-update-slice_fusion.17
  112.8 2.5 dynamic-slice_dynamic-update-slice_fusion.18
  115.4 2.5 dynamic-slice_dynamic-update-slice_fusion.19
  117.9 1.3 dynamic-slice_dynamic-update-slice_fusion.20
  119.2 1.3 dynamic-slice_dynamic-update-slice_fusion.21
  120.5 1.3 dynamic-slice_dynamic-update-slice_fusion.22
  121.8 1.3 dynamic-slice_dynamic-update-slice_fusion.23
  123.2 1.7 constant_dynamic-slice_fusion.2
  124.9 6.1 %convolution_add_fusion.2 = f32[1024,256]{1,0:T(8,128)S(1)} fusion(bf16[1024,4096]{1,0:T(8,128)(2,1)} %dynamic-slice_dynamic-update-slice_fusion.23, bf16[4096,256]{1,0:T(8,128)(2,1)S(1)} %bitcast.9, f32[1024,256]{1,0:T(8,128)S(1)} %get-tuple-element.262, pred[]{:T(512)S(6)} %compare.3), kind=kOutput, calls=%fused_computation.clone.1 | convolution fusion | flops 2148007936 | bytes 12582913 | tf_op jit(solution)/shard_map/while/body/eval_jaxpr/dot_general | solution.py:70
  131.0 2.5 dynamic-slice_dynamic-update-slice_fusion.16
  133.6 2.5 dynamic-slice_dynamic-update-slice_fusion.17
  136.0 2.5 dynamic-slice_dynamic-update-slice_fusion.18
  138.6 2.5 dynamic-slice_dynamic-update-slice_fusion.19
  141.1 1.3 dynamic-slice_dynamic-update-slice_fusion.20
  142.4 1.3 dynamic-slice_dynamic-update-slice_fusion.21
  143.7 1.3 dynamic-slice_dynamic-update-slice_fusion.22
  145.0 1.3 dynamic-slice_dynamic-update-slice_fusion.23
  146.4 1.7 constant_dynamic-slice_fusion.2
  148.1 6.1 %convolution_add_fusion.2 = f32[1024,256]{1,0:T(8,128)S(1)} fusion(bf16[1024,4096]{1,0:T(8,128)(2,1)} %dynamic-slice_dynamic-update-slice_fusion.23, bf16[4096,256]{1,0:T(8,128)(2,1)S(1)} %bitcast.9, f32[1024,256]{1,0:T(8,128)S(1)} %get-tuple-element.262, pred[]{:T(512)S(6)} %compare.3), kind=kOutput, calls=%fused_computation.clone.1 | convolution fusion | flops 2148007936 | bytes 12582913 | tf_op jit(solution)/shard_map/while/body/eval_jaxpr/dot_general | solution.py:70
  154.2 1.0 copy-done.1
  155.2 146.5 %reduce-scatter.2.cloned.1.call-done = f32[16,256]{1,0:T(8,128)} async-done(((f32[1024,256]{1,0:T(8,128)}), f32[16,256]{1,0:T(8,128)}) %reduce-scatter.2.cloned.1.call-update) | async-done | bytes 16400 | tf_op jit(solution)/shard_map/reduce_scatter | solution.py:72
  301.8 1.3 convert_element_type.3
  (15 shorter events, 1.0 us)
Async XLA Ops:
  6.5 101.3 %all-gather.2.cloned.1.call-start = ((), (), s32[]{:S(2)}) async-start(), calls=%async_computation.1 | async-start | bytes 2129920 | tf_op jit(solution)/shard_map/all_gather | solution.py:52
  7.3 6.7 %collective-permute-start = (bf16[32,128]{1,0:T(8,128)(2,1)S(1)}, bf16[32,128]{1,0:T(8,128)(2,1)S(1)}, u32[]{:S(2)}, u32[]{:S(2)}) collective-permute-start(bf16[32,128]{1,0:T(8,128)(2,1)S(1)} %get-tuple-element.208), channel_id=1, source_target_pairs={{0,64},{64,128},{128,192},{192,256},{256,320},{320,384},{384,448},... | collective-permute-start | bytes 24584 | tf_op jit(solution)/shard_map/ppermute | solution.py:17
  11.5 5.5 %collective-permute-start.1 = (bf16[32,128]{1,0:T(8,128)(2,1)S(1)}, bf16[32,128]{1,0:T(8,128)(2,1)S(1)}, u32[]{:S(2)}, u32[]{:S(2)}) collective-permute-start(bf16[32,128]{1,0:T(8,128)(2,1)S(1)} %get-tuple-element.209), channel_id=1, source_target_pairs={{64,0},{128,64},{192,128},{256,192},{320,256},{384,320},{448,384},... | collective-permute-start | bytes 24584 | tf_op jit(solution)/shard_map/ppermute | solution.py:19
  18.4 283.3 %reduce-scatter.2.cloned.1.call-start = ((), (), s32[]{:S(2)}) async-start(), calls=%async_computation.2 | async-start | bytes 1064960 | tf_op jit(solution)/shard_map/reduce_scatter | solution.py:72
  107.8 10.1 %copy-start = (bf16[2048,512]{1,0:T(8,128)(2,1)S(1)}, bf16[2048,512]{1,0:T(8,128)(2,1)}, u32[]{:S(2)}) copy-start(bf16[2048,512]{1,0:T(8,128)(2,1)} %get-tuple-element.282) | copy-start | bytes 6291460 | tf_op jit(solution)/shard_map/while
  131.0 10.1 %copy-start = (bf16[2048,512]{1,0:T(8,128)(2,1)S(1)}, bf16[2048,512]{1,0:T(8,128)(2,1)}, u32[]{:S(2)}) copy-start(bf16[2048,512]{1,0:T(8,128)(2,1)} %get-tuple-element.282) | copy-start | bytes 6291460 | tf_op jit(solution)/shard_map/while
  154.2 1.0 copy-start.1
Sparse Core Ops, SparseCore 0:
  18.5 89.2 all-gather.1
  155.3 146.3 reduce-scatter.1
where the time goes:
time: 311 us; the launch traced here: 310 us
  waiting for transfers between devices  232 us (75%)
  local copies, waits for them, and re-layouts  35.8 us (12%)
  between operations  13.5 us (4%)
  matrix products  12.2 us (4%)
  other arithmetic  9.8 us (3%)
  starting transfers between devices  6.77 us (2%)
    reduce_scatter x1, waiting for transfers between devices, per_device(): lax.psum_scatter(lax.fori_loop(0, block_count, add_block, jnp.zeros((lax....  147 us
    all_gather x1, waiting for transfers between devices, per_device(): history = lax.all_gather(widened, 'tm', axis=0, tiled=True)  82.2 us
    while x18, local copies, waits for them, and re-layouts  28 us
    dot_general x2, matrix products, add_block(): jnp.dot(stacked, tap_panel, preferred_element_type=jnp.float32)  12.2 us
  transfers between devices with their start and end apart: 4, of which 3 were waited for; matrix products, arithmetic and copies ran while one was open for 2% of the time, Pallas kernels for 0%

commit v1 on v0

--- a/solution.py
+++ b/solution.py
@@ -49,7 +49,9 @@
     first_tap = lax.axis_index("tm") * tap_dev
     weights = masked_weights(responses, tap_counts, panel_links, first_tap)
     widened = extended(driven_wave, (("band", 1),), half_width)
-    history = lax.all_gather(widened, "tm", axis=0, tiled=True)
+    history = jnp.concatenate(
+        lax.all_to_all(jnp.stack([widened] * lax.axis_size("tm")), "tm", 0, 0), axis=0
+    )
     block_count = tap_dev // 8
     first_row = jnp.int32(0)
 

time: 311 us -> 286 us (0.920)
  waiting for transfers between devices: 232 us -> 197 us
  starting transfers between devices: 6.77 us -> 22.4 us
  local copies, waits for them, and re-layouts: 35.8 us -> 29.9 us
    all_gather x1 -> x0, waiting for transfers between devices: 82.2 us -> none  [per_device(): history = lax.all_gather(widened, 'tm', axis=0, tiled=True)]
    all_to_all x0 -> x1, waiting for transfers between devices: none -> 44.8 us  [per_device(): lax.all_to_all(jnp.stack([widened] * lax.axis_size('tm')), 'tm', 0, 0)]
    all_to_all x0 -> x1, starting transfers between devices: none -> 15.7 us  [per_device(): lax.all_to_all(jnp.stack([widened] * lax.axis_size('tm')), 'tm', 0, 0)]
    while x18 -> x14, local copies, waits for them, and re-layouts: 28 us -> 18 us
where the time goes in v1:
time: 286 us
  waiting for transfers between devices  197 us (69%)
  local copies, waits for them, and re-layouts  29.9 us (10%)
  starting transfers between devices  22.4 us (8%)
  between operations  13.5 us (5%)
  matrix products  13.4 us (5%)
  other arithmetic  9.19 us (3%)
    reduce_scatter x1, waiting for transfers between devices, per_device(): lax.psum_scatter(lax.fori_loop(0, block_count, add_block, jnp.zeros((lax....  150 us
    all_to_all x1, waiting for transfers between devices, per_device(): lax.all_to_all(jnp.stack([widened] * lax.axis_size('tm')), 'tm', 0, 0)  44.8 us
    while x14, local copies, waits for them, and re-layouts  18 us
    all_to_all x1, starting transfers between devices, per_device(): lax.all_to_all(jnp.stack([widened] * lax.axis_size('tm')), 'tm', 0, 0)  15.7 us
    dot_general x2, matrix products, add_block(): jnp.dot(stacked, tap_panel, preferred_element_type=jnp.float32)  13.4 us
    dynamic_slice x2, local copies, waits for them, and re-layouts, add_block(): lax.dynamic_slice_in_dim(weights, lead_tap, 8, 0)  6.1 us
  transfers between devices with their start and end apart: 4, of which 3 were waited for; matrix products, arithmetic and copies ran while one was open for 2% of the time, Pallas kernels for 0%

profile of v1, /device:TPU:2, one launch (start us, length us, event | category | flops | bytes accessed | tf_op | source)
XLA Modules:
  0.0 285.9 jit_solution(597283215398536425)
XLA Ops:
  7.3 4.3 %collective-permute-start = (bf16[32,128]{1,0:T(8,128)(2,1)S(1)}, bf16[32,128]{1,0:T(8,128)(2,1)S(1)}, u32[]{:S(2)}, u32[]{:S(2)}) collective-permute-start(bf16[32,128]{1,0:T(8,128)(2,1)S(1)} %get-tuple-element.208), channel_id=1, source_target_pairs={{0,64},{64,128},{128,192},{192,256},{256,320},{320,384},{384,448},... | collective-permute-start | bytes 24584 | tf_op jit(solution)/shard_map/ppermute | solution.py:17
  11.5 2.5 collective-permute-start.1
  14.0 3.1 %collective-permute-done.1 = bf16[32,128]{1,0:T(8,128)(2,1)S(1)} collective-permute-done((bf16[32,128]{1,0:T(8,128)(2,1)S(1)}, bf16[32,128]{1,0:T(8,128)(2,1)S(1)}, u32[]{:S(2)}, u32[]{:S(2)}) %collective-permute-start.1) | collective-permute-done | bytes 8224 | tf_op jit(solution)/shard_map/ppermute | solution.py:19
  17.8 1.6 stack.2
  19.4 15.7 %all-to-all-start = ((bf16[64,32,512]{2,1,0:T(8,128)(2,1)}), bf16[64,32,512]{2,1,0:T(8,128)(2,1)S(1)}, u32[]{:S(2)}, u32[]{:S(2)}) async-start(bf16[64,32,512]{2,1,0:T(8,128)(2,1)} %stack.2), calls=%async_computation | async-start | bytes 4194304 | tf_op jit(solution)/shard_map/all_to_all | solution.py:53
  35.2 0.8 compare_reduce_fusion.1
  36.9 5.4 %and_select_fusion = bf16[16,512,256]{2,1,0:T(8,128)(2,1)} fusion(bf16[16,512,256]{2,1,0:T(8,128)(2,1)} %param.7, pred[512,256]{1,0:T(8,128)(4,1)S(1)} %select_select_fusion, pred[16,256]{1,0:T(8,128)(4,1)S(1)} %broadcast_compare_fusion), kind=kLoop, calls=%fused_computation.10 | loop fusion | flops 4194304 | bytes 8523776 | tf_op jit(solution)/shard_map/jit(_where)/select_n | solution.py:40
  42.3 44.8 %all-to-all-done = bf16[64,32,512]{2,1,0:T(8,128)(2,1)S(1)} async-done(((bf16[64,32,512]{2,1,0:T(8,128)(2,1)}), bf16[64,32,512]{2,1,0:T(8,128)(2,1)S(1)}, u32[]{:S(2)}, u32[]{:S(2)}) %all-to-all-start) | async-done | bytes 2097184 | tf_op jit(solution)/shard_map/all_to_all | solution.py:53
  87.1 40.1 %while.18 = (s32[]{:T(128)}, f32[1024,256]{1,0:T(8,128)S(1)}, s32[]{:T(128)}, bf16[2048,512]{1,0:T(8,128)(2,1)S(1)}, bf16[16,512,256]{2,1,0:T(8,128)(2,1)}, /*in...) while((s32[]{:T(128)}, f32[1024,256]{1,0:T(8,128)S(1)}, ...), condition=%wide.region_1.2_spmd.clone, body=%wide.region_0.1_spmd.clone.sunk | while | flops 2148007936 | bytes 33554828 | solution.py:75
  87.1 1.2 dynamic-slice_dynamic-update-slice_fusion.16
  88.2 1.3 dynamic-slice_dynamic-update-slice_fusion.17
  89.5 1.3 dynamic-slice_dynamic-update-slice_fusion.18
  90.8 1.3 dynamic-slice_dynamic-update-slice_fusion.19
  92.2 1.3 dynamic-slice_dynamic-update-slice_fusion.20
  93.5 1.3 dynamic-slice_dynamic-update-slice_fusion.21
  94.8 1.3 dynamic-slice_dynamic-update-slice_fusion.22
  96.1 1.3 dynamic-slice_dynamic-update-slice_fusion.23
  97.4 3.1 %constant_dynamic-slice_fusion.2 = bf16[8,512,256]{2,1,0:T(8,128)(2,1)} fusion(bf16[16,512,256]{2,1,0:T(8,128)(2,1)} %get-tuple-element.283, s32[]{:T(128)S(6)} %select_n.57), kind=kLoop, calls=%fused_computation.9.clone.1 | loop fusion | bytes 4194308 | tf_op jit(solution)/shard_map/while/body/eval_jaxpr/dynamic_slice | solution.py:69
  100.4 6.7 %convolution_add_fusion.2 = f32[1024,256]{1,0:T(8,128)S(1)} fusion(bf16[1024,4096]{1,0:T(8,128)(2,1)} %dynamic-slice_dynamic-update-slice_fusion.23, bf16[4096,256]{1,0:T(8,128)(2,1)} %bitcast.11, f32[1024,256]{1,0:T(8,128)S(1)} %get-tuple-element.262, pred[]{:T(512)S(6)} %compare.3), kind=kOutput, calls=%fused_computation.clone.1 | convolution fusion | flops 2148007936 | bytes 12582913 | tf_op jit(solution)/shard_map/while/body/eval_jaxpr/dot_general | solution.py:72
  107.2 1.2 dynamic-slice_dynamic-update-slice_fusion.16
  108.3 1.3 dynamic-slice_dynamic-update-slice_fusion.17
  109.6 1.3 dynamic-slice_dynamic-update-slice_fusion.18
  110.9 1.3 dynamic-slice_dynamic-update-slice_fusion.19
  112.3 1.3 dynamic-slice_dynamic-update-slice_fusion.20
  113.6 1.3 dynamic-slice_dynamic-update-slice_fusion.21
  114.8 1.3 dynamic-slice_dynamic-update-slice_fusion.22
  116.2 1.3 dynamic-slice_dynamic-update-slice_fusion.23
  117.4 3.1 %constant_dynamic-slice_fusion.2 = bf16[8,512,256]{2,1,0:T(8,128)(2,1)} fusion(bf16[16,512,256]{2,1,0:T(8,128)(2,1)} %get-tuple-element.283, s32[]{:T(128)S(6)} %select_n.57), kind=kLoop, calls=%fused_computation.9.clone.1 | loop fusion | bytes 4194308 | tf_op jit(solution)/shard_map/while/body/eval_jaxpr/dynamic_slice | solution.py:69
  120.5 6.7 %convolution_add_fusion.2 = f32[1024,256]{1,0:T(8,128)S(1)} fusion(bf16[1024,4096]{1,0:T(8,128)(2,1)} %dynamic-slice_dynamic-update-slice_fusion.23, bf16[4096,256]{1,0:T(8,128)(2,1)} %bitcast.11, f32[1024,256]{1,0:T(8,128)S(1)} %get-tuple-element.262, pred[]{:T(512)S(6)} %compare.3), kind=kOutput, calls=%fused_computation.clone.1 | convolution fusion | flops 2148007936 | bytes 12582913 | tf_op jit(solution)/shard_map/while/body/eval_jaxpr/dot_general | solution.py:72
  127.2 1.0 copy-done
  128.2 149.5 %reduce-scatter.2.cloned.1.call-done = f32[16,256]{1,0:T(8,128)} async-done(((f32[1024,256]{1,0:T(8,128)}), f32[16,256]{1,0:T(8,128)}) %reduce-scatter.2.cloned.1.call-update) | async-done | bytes 16400 | tf_op jit(solution)/shard_map/reduce_scatter | solution.py:74
  277.7 1.3 convert_element_type.3
  (11 shorter events, 2.5 us)
Async XLA Ops:
  7.3 6.7 %collective-permute-start = (bf16[32,128]{1,0:T(8,128)(2,1)S(1)}, bf16[32,128]{1,0:T(8,128)(2,1)S(1)}, u32[]{:S(2)}, u32[]{:S(2)}) collective-permute-start(bf16[32,128]{1,0:T(8,128)(2,1)S(1)} %get-tuple-element.208), channel_id=1, source_target_pairs={{0,64},{64,128},{128,192},{192,256},{256,320},{320,384},{384,448},... | collective-permute-start | bytes 24584 | tf_op jit(solution)/shard_map/ppermute | solution.py:17
  11.5 5.5 %collective-permute-start.1 = (bf16[32,128]{1,0:T(8,128)(2,1)S(1)}, bf16[32,128]{1,0:T(8,128)(2,1)S(1)}, u32[]{:S(2)}, u32[]{:S(2)}) collective-permute-start(bf16[32,128]{1,0:T(8,128)(2,1)S(1)} %get-tuple-element.209), channel_id=1, source_target_pairs={{64,0},{128,64},{192,128},{256,192},{320,256},{384,320},{448,384},... | collective-permute-start | bytes 24584 | tf_op jit(solution)/shard_map/ppermute | solution.py:19
  19.4 67.7 %all-to-all-start = ((bf16[64,32,512]{2,1,0:T(8,128)(2,1)}), bf16[64,32,512]{2,1,0:T(8,128)(2,1)S(1)}, u32[]{:S(2)}, u32[]{:S(2)}) async-start(bf16[64,32,512]{2,1,0:T(8,128)(2,1)} %stack.2), calls=%async_computation | async-start | bytes 4194304 | tf_op jit(solution)/shard_map/all_to_all | solution.py:53
  35.1 242.7 %reduce-scatter.2.cloned.1.call-start = ((), (), s32[]{:S(2)}) async-start(), calls=%async_computation.2 | async-start | bytes 1064960 | tf_op jit(solution)/shard_map/reduce_scatter | solution.py:74
  127.2 1.0 copy-start
Sparse Core Ops, SparseCore 0:
  128.3 149.3 reduce-scatter.1
